TPU v7x, 32 devices: a whole 2x2x4 slice. The times are simulated.
32 devices in a mesh: seq: 4 (over y, x), ctx: 8 (over z, core).
Axes of the slice: x: 2, y: 2, z: 4, core: 2. Of those that a mesh axis runs over, the one named last changes fastest.
Arguments:
- hidden_in: bfloat16 [16, 1024, 768], P('seq', 'ctx'), may hold values from -6 to 6
- cotangent: bfloat16 [16, 1024, 768], P('seq', 'ctx'), may hold values from -6 to 6
- segments: int32 [16, 1024], P('seq', 'ctx'), may hold values from 0 to 3, never falling along the last dimension, each value on 1 to 512 neighbouring positions
- qkv_weight: bfloat16 [768, 2304], P('seq'), may hold values from -0.21875 to 0.21875
- query_bias: bfloat16 [768], P('seq'), may hold values from -3 to 3
- value_bias: bfloat16 [768], P('seq'), may hold values from -0.29882812 to 0.29882812
- out_weight: bfloat16 [768, 768], P('seq'), may hold values from -1.75 to 1.75
- out_bias: bfloat16 [768], P('seq'), may hold values from -2 to 2
- first_gain: bfloat16 [768], P('seq'), may hold values from 0.5 to 1.5
- first_shift: bfloat16 [768], P('seq'), may hold values from -2 to 2
- inner_weight: bfloat16 [768, 3072], P('seq'), may hold values from -0.21875 to 0.21875
- inner_bias: bfloat16 [3072], P('seq'), may hold values from -3 to 3
- outer_weight: bfloat16 [3072, 768], P('seq'), may hold values from -0.21875 to 0.21875
- outer_bias: bfloat16 [768], P('seq'), may hold values from -2 to 2
- second_gain: bfloat16 [768], P('seq'), may hold values from 0.5 to 1.5
- second_shift: bfloat16 [768], P('seq'), may hold values from -2 to 2
Outputs:
- output: bfloat16 [16, 1024, 768], P('seq', 'ctx')
- grad_input: float32 [16, 1024, 768], P('seq', 'ctx')
- grad_qkv_weight: float32 [768, 2304], P('seq')
- grad_query_bias: float32 [768], P('seq')
- grad_value_bias: float32 [768], P('seq')
- grad_out_weight: float32 [768, 768], P('seq')
- grad_out_bias: float32 [768], P('seq')
- grad_first_gain: float32 [768], P('seq')
- grad_first_shift: float32 [768], P('seq')
- grad_inner_weight: float32 [768, 3072], P('seq')
- grad_inner_bias: float32 [3072], P('seq')
- grad_outer_weight: float32 [3072, 768], P('seq')
- grad_outer_bias: float32 [768], P('seq')
- grad_second_gain: float32 [768], P('seq')
- grad_second_shift: float32 [768], P('seq')
Inputs may be any that keep to these rules, and one draw needn't show every extreme that they name: `segments`: in each sequence the document numbers never fall along the positions; a document holds 1 to 512 positions, and some document holds exactly 512; attention joins only positions of one document of one sequence.
All inputs are finite; a program needn't handle non-finite values.
Results may differ from a plain program's by a relative error of at most 0.035.
Values may be sent and summed in bfloat16 or wider, within the bound.
A program may use at most 320 MiB of HBM per device.

v0:
```python
from functools import partial
import jax
import jax.numpy as jnp
from jax import lax
from jax.sharding import PartitionSpec as P

HEADS = 12
HEAD_DIM = 64
norm_epsilon = 1e-12


def norm_forward(matrix, gain, shift):
    average = jnp.mean(matrix, axis=-1, keepdims=True)
    centred = matrix - average
    factor = lax.rsqrt(jnp.mean(centred * centred, axis=-1, keepdims=True) + norm_epsilon)
    normed = centred * factor
    return (normed * gain + shift, normed, factor)


def norm_backward(upstream, normed, factor, gain):
    scaled = upstream * gain
    return factor * (
        scaled
        - jnp.mean(scaled, axis=-1, keepdims=True)
        - normed * jnp.mean(scaled * normed, axis=-1, keepdims=True)
    )


def split_heads(matrix):
    groups, positions, widths = matrix.shape
    return jnp.moveaxis(matrix.reshape(groups, positions, HEADS, widths // HEADS), 2, 0)


def join_heads(matrix):
    return jnp.moveaxis(matrix, 0, 2).reshape(
        matrix.shape[1], matrix.shape[2], matrix.shape[0] * matrix.shape[3]
    )


def grads_block(query_one, upstream_one, lse_one, delta_one, key_one, value_one, allowed, scaling):
    scores = (
        jnp.einsum("sqd,skd->sqk", query_one, key_one, preferred_element_type=jnp.float32) * scaling
    )
    probability = jnp.exp(jnp.where(allowed, scores - lse_one[..., None], -1e30))
    grad_probs = jnp.einsum(
        "sqd,skd->sqk", upstream_one, value_one, preferred_element_type=jnp.float32
    )
    grad_scores = (probability * (grad_probs - delta_one[..., None])).astype(jnp.bfloat16)
    grad_query = (
        jnp.einsum("sqk,skd->sqd", grad_scores, key_one, preferred_element_type=jnp.float32)
        * scaling
    )
    grad_key = (
        jnp.einsum("sqk,sqd->skd", grad_scores, query_one, preferred_element_type=jnp.float32)
        * scaling
    )
    grad_value = jnp.einsum(
        "sqk,sqd->skd",
        probability.astype(jnp.bfloat16),
        upstream_one,
        preferred_element_type=jnp.float32,
    )
    return (grad_query, grad_key, grad_value)


def on_device(
    hidden_in,
    cotangent,
    segments,
    qkv_weight,
    query_bias,
    value_bias,
    out_weight,
    out_bias,
    first_gain,
    first_shift,
    inner_weight,
    inner_bias,
    outer_weight,
    outer_bias,
    second_gain,
    second_shift,
):
    groups, positions, model_width = hidden_in.shape
    row_count = groups * positions
    scaling = HEAD_DIM ** (-0.5)
    gathered = (
        lax.all_gather(qkv_weight, "seq", axis=0, tiled=True),
        lax.all_gather(query_bias, "seq", axis=0, tiled=True),
        lax.all_gather(value_bias, "seq", axis=0, tiled=True),
        lax.all_gather(out_weight, "seq", axis=0, tiled=True),
        lax.all_gather(out_bias, "seq", axis=0, tiled=True),
        lax.all_gather(first_gain, "seq", axis=0, tiled=True),
        lax.all_gather(first_shift, "seq", axis=0, tiled=True),
        lax.all_gather(inner_weight, "seq", axis=0, tiled=True),
        lax.all_gather(inner_bias, "seq", axis=0, tiled=True),
        lax.all_gather(outer_weight, "seq", axis=0, tiled=True),
        lax.all_gather(outer_bias, "seq", axis=0, tiled=True),
        lax.all_gather(second_gain, "seq", axis=0, tiled=True),
        lax.all_gather(second_shift, "seq", axis=0, tiled=True),
    )
    (
        qkv_full,
        qbias_full,
        vbias_full,
        out_full,
        obias_full,
        fgain_full,
        fshift_full,
        inner_full,
        ibias_full,
        outer_full,
        ubias_full,
        sgain_full,
        sshift_full,
    ) = gathered
    token_rows = hidden_in.reshape(row_count, model_width)
    projected = jnp.dot(token_rows, qkv_full, preferred_element_type=jnp.float32)
    queries_low = (
        (projected[:, :model_width] + qbias_full)
        .astype(jnp.bfloat16)
        .reshape(groups, positions, model_width)
    )
    keys_low = (
        projected[:, model_width : 2 * model_width]
        .astype(jnp.bfloat16)
        .reshape(groups, positions, model_width)
    )
    values_low = (
        (projected[:, 2 * model_width :] + vbias_full)
        .astype(jnp.bfloat16)
        .reshape(groups, positions, model_width)
    )
    seg_low = segments.astype(jnp.bfloat16)
    query_heads = split_heads(queries_low)
    start_state = (
        jnp.full((HEADS, groups, positions), -1e30, jnp.float32),
        jnp.zeros((HEADS, groups, positions), jnp.float32),
        jnp.zeros((HEADS, groups, positions, HEAD_DIM), jnp.float32),
    )
    key_part = lax.all_gather(keys_low, "ctx", axis=1, tiled=True)
    value_part = lax.all_gather(values_low, "ctx", axis=1, tiled=True)
    seg_part = lax.all_gather(seg_low, "ctx", axis=1, tiled=True)
    fold_allowed = seg_low[:, :, None] == seg_part[:, None, :]

    def per_head(head_item):
        query_one, key_one, value_one, old_max, old_total, old_acc = head_item
        scores = (
            jnp.einsum("sqd,skd->sqk", query_one, key_one, preferred_element_type=jnp.float32)
            * scaling
        )
        scores = jnp.where(fold_allowed, scores, -1e30)
        new_max = jnp.maximum(old_max, jnp.max(scores, axis=-1))
        retain = jnp.exp(old_max - new_max)
        weights = jnp.where(fold_allowed, jnp.exp(scores - new_max[..., None]), 0.0)
        run_total = old_total * retain + jnp.sum(weights, axis=-1)
        run_acc = old_acc * retain[..., None] + jnp.einsum(
            "sqk,skd->sqd",
            weights.astype(jnp.bfloat16),
            value_one,
            preferred_element_type=jnp.float32,
        )
        return (new_max, run_total, run_acc)

    run_max, run_total, run_acc = lax.map(
        per_head,
        (
            query_heads,
            split_heads(key_part),
            split_heads(value_part),
            start_state[0],
            start_state[1],
            start_state[2],
        ),
    )
    out_heads = run_acc / run_total[..., None]
    row_lse = run_max + jnp.log(run_total)
    context_low = join_heads(out_heads).reshape(row_count, model_width).astype(jnp.bfloat16)
    attended = jnp.dot(context_low, out_full, preferred_element_type=jnp.float32) + obias_full
    residual = token_rows.astype(jnp.float32) + attended
    first, first_normed, first_factor = norm_forward(residual, fgain_full, fshift_full)
    first_low = first.astype(jnp.bfloat16)
    inner = jnp.dot(first_low, inner_full, preferred_element_type=jnp.float32) + ibias_full
    active = jax.nn.gelu(inner, approximate=False).astype(jnp.bfloat16)
    branch = jnp.dot(active, outer_full, preferred_element_type=jnp.float32) + ubias_full
    result, second_normed, second_factor = norm_forward(first + branch, sgain_full, sshift_full)
    output = result.astype(jnp.bfloat16).reshape(groups, positions, model_width)
    qkv_back, out_back, inner_back, outer_back, fgain_back, sgain_back = (
        lax.all_gather(qkv_weight, "seq", axis=0, tiled=True),
        lax.all_gather(out_weight, "seq", axis=0, tiled=True),
        lax.all_gather(inner_weight, "seq", axis=0, tiled=True),
        lax.all_gather(outer_weight, "seq", axis=0, tiled=True),
        lax.all_gather(first_gain, "seq", axis=0, tiled=True),
        lax.all_gather(second_gain, "seq", axis=0, tiled=True),
    )
    grad_out = cotangent.reshape(row_count, model_width).astype(jnp.float32)
    grad_second_gain = jnp.sum(grad_out * second_normed, axis=0)
    grad_second_shift = jnp.sum(grad_out, axis=0)
    grad_second = norm_backward(grad_out, second_normed, second_factor, sgain_back)
    grad_branch = grad_second.astype(jnp.bfloat16)
    grad_outer_weight = jnp.einsum(
        "rf,rd->fd", active, grad_branch, preferred_element_type=jnp.float32
    )
    grad_outer_bias = jnp.sum(grad_branch.astype(jnp.float32), axis=0)
    grad_active = jnp.einsum(
        "rd,fd->rf", grad_branch, outer_back, preferred_element_type=jnp.float32
    )
    _, gelu_pull = jax.vjp(partial(jax.nn.gelu, approximate=False), inner)
    grad_inner = gelu_pull(grad_active)[0].astype(jnp.bfloat16)
    grad_inner_weight = jnp.einsum(
        "rd,rf->df", first_low, grad_inner, preferred_element_type=jnp.float32
    )
    grad_inner_bias = jnp.sum(grad_inner.astype(jnp.float32), axis=0)
    grad_first = grad_second + jnp.einsum(
        "rf,df->rd", grad_inner, inner_back, preferred_element_type=jnp.float32
    )
    grad_first_gain = jnp.sum(grad_first * first_normed, axis=0)
    grad_first_shift = jnp.sum(grad_first, axis=0)
    grad_residual = norm_backward(grad_first, first_normed, first_factor, fgain_back)
    grad_attended = grad_residual.astype(jnp.bfloat16)
    grad_out_weight = jnp.einsum(
        "rd,re->de", context_low, grad_attended, preferred_element_type=jnp.float32
    )
    grad_out_bias = jnp.sum(grad_attended.astype(jnp.float32), axis=0)
    grad_context = jnp.einsum(
        "re,de->rd", grad_attended, out_back, preferred_element_type=jnp.float32
    )
    grad_context = grad_context.astype(jnp.bfloat16).reshape(groups, positions, model_width)
    grad_heads = split_heads(grad_context)
    row_delta = jnp.sum(grad_heads.astype(jnp.float32) * out_heads, axis=-1)
    far_keys, far_values, far_segs = (
        lax.all_gather(keys_low, "ctx", axis=1, tiled=True),
        lax.all_gather(values_low, "ctx", axis=1, tiled=True),
        lax.all_gather(seg_low, "ctx", axis=1, tiled=True),
    )
    allowed = seg_low[:, :, None] == far_segs[:, None, :]

    def head_keys(head_item):
        query_one, upstream_one, lse_one, delta_one, key_one, value_one = head_item
        return grads_block(
            query_one, upstream_one, lse_one, delta_one, key_one, value_one, allowed, scaling
        )

    dq_heads, dk_heads, dv_heads = lax.map(
        head_keys,
        (
            query_heads,
            grad_heads,
            row_lse,
            row_delta,
            split_heads(far_keys),
            split_heads(far_values),
        ),
    )
    key_grad, value_grad = (
        lax.psum_scatter(
            join_heads(dk_heads).astype(jnp.bfloat16), "ctx", scatter_dimension=1, tiled=True
        ).astype(jnp.float32),
        lax.psum_scatter(
            join_heads(dv_heads).astype(jnp.bfloat16), "ctx", scatter_dimension=1, tiled=True
        ).astype(jnp.float32),
    )
    query_grad = join_heads(dq_heads)
    query_low_grad = query_grad.reshape(row_count, model_width).astype(jnp.bfloat16)
    key_low_grad = key_grad.reshape(row_count, model_width).astype(jnp.bfloat16)
    value_low_grad = value_grad.reshape(row_count, model_width).astype(jnp.bfloat16)
    grad_projected = jnp.concatenate([query_low_grad, key_low_grad, value_low_grad], axis=1)
    grad_qkv_weight = jnp.einsum(
        "rd,rf->df", token_rows, grad_projected, preferred_element_type=jnp.float32
    )
    grad_query_bias = jnp.sum(query_low_grad.astype(jnp.float32), axis=0)
    grad_value_bias = jnp.sum(value_low_grad.astype(jnp.float32), axis=0)
    grad_input = grad_residual + jnp.einsum(
        "rf,df->rd", grad_projected, qkv_back, preferred_element_type=jnp.float32
    )
    owned = (
        lax.psum_scatter(
            grad_qkv_weight.astype(jnp.bfloat16), "seq", scatter_dimension=0, tiled=True
        ).astype(jnp.float32),
        lax.psum_scatter(
            grad_query_bias.astype(jnp.bfloat16), "seq", scatter_dimension=0, tiled=True
        ).astype(jnp.float32),
        lax.psum_scatter(
            grad_value_bias.astype(jnp.bfloat16), "seq", scatter_dimension=0, tiled=True
        ).astype(jnp.float32),
        lax.psum_scatter(
            grad_out_weight.astype(jnp.bfloat16), "seq", scatter_dimension=0, tiled=True
        ).astype(jnp.float32),
        lax.psum_scatter(
            grad_out_bias.astype(jnp.bfloat16), "seq", scatter_dimension=0, tiled=True
        ).astype(jnp.float32),
        lax.psum_scatter(
            grad_first_gain.astype(jnp.bfloat16), "seq", scatter_dimension=0, tiled=True
        ).astype(jnp.float32),
        lax.psum_scatter(
            grad_first_shift.astype(jnp.bfloat16), "seq", scatter_dimension=0, tiled=True
        ).astype(jnp.float32),
        lax.psum_scatter(
            grad_inner_weight.astype(jnp.bfloat16), "seq", scatter_dimension=0, tiled=True
        ).astype(jnp.float32),
        lax.psum_scatter(
            grad_inner_bias.astype(jnp.bfloat16), "seq", scatter_dimension=0, tiled=True
        ).astype(jnp.float32),
        lax.psum_scatter(
            grad_outer_weight.astype(jnp.bfloat16), "seq", scatter_dimension=0, tiled=True
        ).astype(jnp.float32),
        lax.psum_scatter(
            grad_outer_bias.astype(jnp.bfloat16), "seq", scatter_dimension=0, tiled=True
        ).astype(jnp.float32),
        lax.psum_scatter(
            grad_second_gain.astype(jnp.bfloat16), "seq", scatter_dimension=0, tiled=True
        ).astype(jnp.float32),
        lax.psum_scatter(
            grad_second_shift.astype(jnp.bfloat16), "seq", scatter_dimension=0, tiled=True
        ).astype(jnp.float32),
    )
    summed = (
        lax.psum(owned[0].astype(jnp.bfloat16), "ctx").astype(jnp.float32),
        lax.psum(owned[1].astype(jnp.bfloat16), "ctx").astype(jnp.float32),
        lax.psum(owned[2].astype(jnp.bfloat16), "ctx").astype(jnp.float32),
        lax.psum(owned[3].astype(jnp.bfloat16), "ctx").astype(jnp.float32),
        lax.psum(owned[4].astype(jnp.bfloat16), "ctx").astype(jnp.float32),
        lax.psum(owned[5].astype(jnp.bfloat16), "ctx").astype(jnp.float32),
        lax.psum(owned[6].astype(jnp.bfloat16), "ctx").astype(jnp.float32),
        lax.psum(owned[7].astype(jnp.bfloat16), "ctx").astype(jnp.float32),
        lax.psum(owned[8].astype(jnp.bfloat16), "ctx").astype(jnp.float32),
        lax.psum(owned[9].astype(jnp.bfloat16), "ctx").astype(jnp.float32),
        lax.psum(owned[10].astype(jnp.bfloat16), "ctx").astype(jnp.float32),
        lax.psum(owned[11].astype(jnp.bfloat16), "ctx").astype(jnp.float32),
        lax.psum(owned[12].astype(jnp.bfloat16), "ctx").astype(jnp.float32),
    )
    return (
        output,
        grad_input.reshape(groups, positions, model_width),
        summed[0],
        summed[1],
        summed[2],
        summed[3],
        summed[4],
        summed[5],
        summed[6],
        summed[7],
        summed[8],
        summed[9],
        summed[10],
        summed[11],
        summed[12],
    )


def solution(mesh):
    placed = (
        P("seq", "ctx", None),
        P("seq", "ctx", None),
        P("seq", "ctx"),
        P("seq", None),
        P("seq"),
        P("seq"),
        P("seq", None),
        P("seq"),
        P("seq"),
        P("seq"),
        P("seq", None),
        P("seq"),
        P("seq", None),
        P("seq"),
        P("seq"),
        P("seq"),
    )
    return jax.shard_map(
        on_device,
        mesh=mesh,
        in_specs=placed,
        out_specs=(
            P("seq", "ctx", None),
            P("seq", "ctx", None),
            P("seq", None),
            P("seq"),
            P("seq"),
            P("seq", None),
            P("seq"),
            P("seq"),
            P("seq"),
            P("seq", None),
            P("seq"),
            P("seq", None),
            P("seq"),
            P("seq"),
            P("seq"),
        ),
        check_vma=False,
    )
```

profile of v0, /device:TPU:0, one launch (start us, length us, event | category | flops | bytes accessed | tf_op | source)
XLA Modules:
  0.0 961.4 jit_solution(5188691105644556815)
XLA Ops:
  15.8 17.8 %all-reduce.20 = (bf16[768]{0:T(1024)(128)(2,1)S(1)}, bf16[768]{0:T(1024)(128)(2,1)S(1)}, bf16[768]{0:T(1024)(128)(2,1)S(1)}, bf16[768]{0:T(1024)(128)(2,1)S(1)}...) all-reduce(bf16[768]{0:T(1024)(128)(2,1)S(1)} %dynamic-update-slice, ...), channel_id=1, replica_groups=mesh['seq'=4,'ctx'=8] {'seq'}, use_global_device_ids=true, to_apply=%add | all-reduce | flops 5376 | bytes 21504
  33.7 26.3 %all-gather.8.cloned.1.call-done = bf16[768,2304]{1,0:T(8,128)(2,1)} async-done(((bf16[192,2304]{1,0:T(8,128)(2,1)}), bf16[768,2304]{1,0:T(8,128)(2,1)}) %all-gather.8.cloned.1.call-update) | async-done | bytes 3538960 | tf_op jit(solution)/shard_map/all_gather | solution.py:88
  60.0 4.3 fusion.86
  72.2 11.9 %all_gather.60 = bf16[4,1024]{1,0:T(4,128)(2,1)S(1)} all-gather(bf16[4,128]{1,0:T(4,128)(2,1)S(1)} %convert_element_type.236), channel_id=1, replica_groups=mesh['seq'=4,'ctx'=8] {'ctx'}, dimensions={1}, use_global_device_ids=true | all-gather | bytes 9216 | tf_op jit(solution)/shard_map/all_gather | solution.py:143
  84.1 8.2 all-gather
  96.5 36.3 %all-gather.12.cloned.1.call-done = bf16[4,1024,768]{1,2,0:T(8,128)(2,1)} async-done(((bf16[4,128,768]{1,2,0:T(8,128)(2,1)}), bf16[4,1024,768]{1,2,0:T(8,128)(2,1)}) %all-gather.12.cloned.1.call-update) | async-done | bytes 6291472 | tf_op jit(solution)/shard_map/all_gather | solution.py:142
  132.9 6.7 copy.57
  139.6 58.8 %all-gather.10.cloned.1.call-done = bf16[4,1024,768]{1,2,0:T(8,128)(2,1)} async-done(((bf16[4,128,768]{1,2,0:T(8,128)(2,1)}), bf16[4,1024,768]{1,2,0:T(8,128)(2,1)}) %all-gather.10.cloned.1.call-update) | async-done | bytes 6291472 | tf_op jit(solution)/shard_map/all_gather | solution.py:141
  198.4 6.7 copy.56
  205.1 51.8 %while.30 = (s32[]{:T(128)}, f32[12,4,128]{2,1,0:T(4,128)S(1)}, f32[12,4,128]{2,1,0:T(4,128)S(1)}, f32[12,4,128,64]{2,1,3,0:T(4,128)S(1)}, bf16[12,4,128,64]{2,3...) while((s32[]{:T(128)}, f32[12,4,128]{2,1,0:T(4,128)S(1)}, ...), condition=%wide.region_3.4_spmd.clone, body=%wide.region_0.3_spmd.clone.sunk | while | flops 142641664 | bytes 7852653 | solution.py:165
  258.0 2.6 fusion.83
  261.0 23.9 %all-gather.16.cloned.1.call-done = bf16[768,3072]{1,0:T(8,128)(2,1)} async-done(((bf16[192,3072]{1,0:T(8,128)(2,1)}), bf16[768,3072]{1,0:T(8,128)(2,1)}) %all-gather.16.cloned.1.call-update) | async-done | bytes 4718608 | tf_op jit(solution)/shard_map/all_gather | solution.py:95
  284.9 19.8 %multiply_convert_fusion.1 = (bf16[512,3072]{1,0:T(8,128)(2,1)}, f32[512,3072]{1,0:T(8,128)}, f32[512,3072]{1,0:T(8,128)}) fusion(f32[3072]{0:T(1024)S(1)} %bitcast.237, bf16[768,3072]{1,0:T(8,128)(2,1)} %all-gather.16.cloned.1.call-done, f32[512,768]{1,0:T(8,128)S(1)} %get-tuple-element.358, f32[768]{0:T(1024)S(1)} %convert_element_type.244, ...), kind=kOutput, calls=%fused_computation.66 | convolution fusion | flops 2521694208 | bytes 22042624 | tf_op jit(solution)/shard_map/dot_general | solution.py:183
  304.7 39.0 %all-gather.18.cloned.1.call-done = bf16[3072,768]{1,0:T(8,128)(2,1)} async-done(((bf16[768,768]{1,0:T(8,128)(2,1)}), bf16[3072,768]{1,0:T(8,128)(2,1)}) %all-gather.18.cloned.1.call-update) | async-done | bytes 4718608 | tf_op jit(solution)/shard_map/all_gather | solution.py:97
  343.7 6.5 fusion.84
  353.2 9.2 fusion.85
  362.4 5.1 multiply_reduce_fusion
  375.0 103.3 %while.31 = (s32[]{:T(128)}, bf16[12,4,128,64]{2,3,1,0:T(8,128)(2,1)}, bf16[12,4,1024,64]{2,3,0,1:T(8,128)(2,1)}, bf16[12,4,1024,64]{2,3,0,1:T(8,128)(2,1)}, bf1...) while((s32[]{:T(128)}, ...), condition=%wide.region_14.15_spmd.clone, body=%wide.region_13.14_spmd.clone.sunk | while | flops 340033536 | bytes 13657221 | solution.py:244
  381.8 2.2 fusion.138
  390.4 2.2 fusion.138
  398.9 2.2 fusion.138
  424.6 2.2 fusion.138
  433.2 2.2 fusion.138
  441.8 2.2 fusion.138
  458.9 2.2 fusion.138
  467.5 2.2 fusion.138
  478.3 10.8 %copy.70 = bf16[4,1024,768]{2,0,1:T(4,128)(2,1)} copy(bf16[4,1024,768]{1,2,0:T(8,128)(2,1)} %bitcast.219) | data formatting | bytes 12582912
  489.0 6.9 copy.100
  496.0 11.0 %copy.72 = bf16[4,1024,768]{2,0,1:T(4,128)(2,1)} copy(bf16[4,1024,768]{1,2,0:T(8,128)(2,1)} %bitcast.220) | data formatting | bytes 12582912
  507.0 7.0 copy.102
  516.8 49.2 %reduce-scatter.19.cloned.1.call-done = bf16[128,3072]{1,0:T(8,128)(2,1)} async-done(((bf16[1024,3072]{1,0:T(8,128)(2,1)}), bf16[128,3072]{1,0:T(8,128)(2,1)}) %reduce-scatter.19.cloned.1.call-update) | async-done | bytes 786448
  569.3 67.2 %reduce-scatter.21.cloned.1.call-done = bf16[128,3072]{1,0:T(8,128)(2,1)} async-done(((bf16[1024,3072]{1,0:T(8,128)(2,1)}), bf16[128,3072]{1,0:T(8,128)(2,1)}) %reduce-scatter.21.cloned.1.call-update) | async-done | bytes 786448
  639.8 2.2 bitcast_dynamic-update-slice_fusion.2
  644.1 5.4 fusion.54
  649.5 5.8 copy.74
  655.4 3.5 convolution_convert_fusion.3
  659.1 7.9 convolution_convert_fusion.1
  667.2 7.4 convolution_convert_fusion
  674.7 26.5 %reduce-scatter.23.cloned.1.call-done = bf16[192,2304]{1,0:T(8,128)(2,1)} async-done(((bf16[768,2304]{1,0:T(8,128)(2,1)}), bf16[192,2304]{1,0:T(8,128)(2,1)}) %reduce-scatter.23.cloned.1.call-update) | async-done | bytes 884752
  701.1 2.3 copy.75
  703.5 29.0 %reduce-scatter.13.cloned.1.call-done = bf16[192,768]{1,0:T(8,128)(2,1)} async-done(((bf16[768,768]{1,0:T(8,128)(2,1)}), bf16[192,768]{1,0:T(8,128)(2,1)}) %reduce-scatter.13.cloned.1.call-update) | async-done | bytes 294928 | tf_op jit(solution)/shard_map/reduce_scatter | solution.py:286
  732.5 60.1 %reduce-scatter.15.cloned.1.call-done = bf16[192,3072]{1,0:T(8,128)(2,1)} async-done(((bf16[768,3072]{1,0:T(8,128)(2,1)}), bf16[192,3072]{1,0:T(8,128)(2,1)}) %reduce-scatter.15.cloned.1.call-update) | async-done | bytes 1179664 | tf_op jit(solution)/shard_map/reduce_scatter | solution.py:298
  792.6 60.0 %reduce-scatter.17.cloned.1.call-done = bf16[768,768]{1,0:T(8,128)(2,1)} async-done(((bf16[3072,768]{1,0:T(8,128)(2,1)}), bf16[768,768]{1,0:T(8,128)(2,1)}) %reduce-scatter.17.cloned.1.call-update) | async-done | bytes 1179664 | tf_op jit(solution)/shard_map/reduce_scatter | solution.py:304
  856.1 15.5 %all-reduce.19 = (bf16[768]{0:T(1024)(128)(2,1)S(1)}, bf16[768]{0:T(1024)(128)(2,1)S(1)}, bf16[768]{0:T(1024)(128)(2,1)S(1)}, bf16[768]{0:T(1024)(128)(2,1)S(1)}...) all-reduce(bf16[768]{0:T(1024)(128)(2,1)S(1)} %dynamic-update-slice, ...), channel_id=1, replica_groups=mesh['seq'=4,'ctx'=8] {'seq'}, use_global_device_ids=true, to_apply=%add.7 | all-reduce | flops 9984 | bytes 39936
  872.3 15.2 %all-reduce.17 = (bf16[192]{0:T(256)(128)(2,1)S(1)}, bf16[192]{0:T(256)(128)(2,1)S(1)}, bf16[192]{0:T(256)(128)(2,1)S(1)}, bf16[192]{0:T(256)(128)(2,1)S(1)}, bf...) all-reduce(bf16[192]{0:T(256)(128)(2,1)S(1)} %dynamic-slice.9, ...), channel_id=1, replica_groups=mesh['seq'=4,'ctx'=8] {'ctx'}, use_global_device_ids=true, to_apply=%region_21.22 | all-reduce | flops 2304 | bytes 9216 | tf_op jit(solution)/shard_map/psum | solution.py:319
  893.8 5.9 convolution_add_fusion.1
  899.7 47.9 %all-reduce.23.cloned.1.call-done = (bf16[192,2304]{0,1:T(8,128)(2,1)}, bf16[192,768]{1,0:T(8,128)(2,1)}, bf16[192,3072]{1,0:T(8,128)(2,1)}, bf16[768,768]{1,0:T(8,128)(2,1)}) async-done(((bf16[192,2304]{0,1:T(8,128)(2,1)}, bf16[192,768]{1,0:T(8,128)(2,1)}, bf16[192,3072]{1,0:T(8,128)(2,1)}, bf16[768,768]{1,0:T(8,128)(2,1)}), (bf16[192,2304]{0,1:T(8,128)(2,1)}, bf16[192,768]{1,0:T(8,128)(2,1)}, ...) | async-done | bytes 3538960 | tf_op jit(solution)/shard_map/psum | solution.py:318
  947.6 3.0 convert_element_type.284
  (309 shorter events, 193.8 us)
Async XLA Ops:
  7.2 52.8 %all-gather.8.cloned.1.call-start = ((), (), s32[]{:S(2)}) async-start(), calls=%async_computation.6 | async-start | bytes 4423680 | tf_op jit(solution)/shard_map/all_gather | solution.py:88
  7.9 125.0 %all-gather.12.cloned.1.call-start = ((), (), s32[]{:S(2)}) async-start(), calls=%async_computation.8 | async-start | bytes 7077888 | tf_op jit(solution)/shard_map/all_gather | solution.py:142
  64.2 2.1 copy-start.6
  67.5 130.9 %all-gather.10.cloned.1.call-start = ((), (), s32[]{:S(2)}) async-start(), calls=%async_computation.7 | async-start | bytes 7077888 | tf_op jit(solution)/shard_map/all_gather | solution.py:141
  69.1 3.1 copy-start.12
  69.1 15.0 %copy-start.13 = (bf16[768]{0:T(1024)(128)(2,1)S(1)}, bf16[768]{0:T(1024)(128)(2,1)}, u32[]{:S(2)}) copy-start(bf16[768]{0:T(1024)(128)(2,1)} %param.31) | copy-start | bytes 4612
  69.1 23.2 %copy-start = (bf16[4,128,768]{2,1,0:T(8,128)(2,1)S(1)}, bf16[4,128,768]{2,1,0:T(8,128)(2,1)}, u32[]{:S(2)}) copy-start(bf16[4,128,768]{2,1,0:T(8,128)(2,1)} %param.21) | copy-start | bytes 2359300
  70.3 187.0 %all-gather.14.cloned.1.call-start = ((), (), s32[]{:S(2)}) async-start(), calls=%async_computation.9 | async-start | bytes 1474560 | tf_op jit(solution)/shard_map/all_gather | solution.py:91
  70.9 214.0 %all-gather.16.cloned.1.call-start = ((), (), s32[]{:S(2)}) async-start(), calls=%async_computation.10 | async-start | bytes 5898240 | tf_op jit(solution)/shard_map/all_gather | solution.py:95
  71.5 272.2 %all-gather.18.cloned.1.call-start = ((), (), s32[]{:S(2)}) async-start(), calls=%async_computation.11 | async-start | bytes 5898240 | tf_op jit(solution)/shard_map/all_gather | solution.py:97
  72.0 493.9 %reduce-scatter.19.cloned.1.call-start = ((), (), s32[]{:S(2)}) async-start(), calls=%async_computation.15 | async-start | bytes 7077888
  256.9 1.1 copy-start.5
  257.2 3.4 copy-start.7
  260.7 44.0 %copy-start.3 = (f32[512,768]{1,0:T(8,128)}, f32[512,768]{1,0:T(8,128)S(1)}, u32[]{:S(2)}) copy-start(f32[512,768]{1,0:T(8,128)S(1)} %get-tuple-element.358) | copy-start | bytes 4718596
  350.5 2.8 copy-start.14
  351.1 11.3 %slice-start = ((s8[4718592]{0:T(1024)(128)(4,1)}), s8[4194304]{0:T(1024)(128)(4,1)S(1)}, s32[]{:S(2)}) async-start(s8[4718592]{0:T(1024)(128)(4,1)} %bitcast.239), calls=%async_computation.19 | async-start | bytes 8388608
  351.7 10.7 %copy-start.8 = (f32[512,768]{1,0:T(8,128)}, f32[512,768]{1,0:T(8,128)S(1)}, u32[]{:S(2)}) copy-start(f32[512,768]{1,0:T(8,128)S(1)} %get-tuple-element.340) | copy-start | bytes 4718596
  353.2 9.2 copy-start.4
  353.2 9.2 slice-start.1
  367.6 1.7 copy-start.15
  368.1 1.1 copy-start.1
  496.0 140.5 %reduce-scatter.21.cloned.1.call-start = ((), (), s32[]{:S(2)}) async-start(), calls=%async_computation.16 | async-start | bytes 7077888
  514.0 187.1 %reduce-scatter.23.cloned.1.call-start = ((), (), s32[]{:S(2)}) async-start(), calls=%async_computation.17 | async-start | bytes 4423680
  639.8 4.3 copy-start.16
  655.4 77.1 %reduce-scatter.13.cloned.1.call-start = ((), (), s32[]{:S(2)}) async-start(), calls=%async_computation.12 | async-start | bytes 1474560 | tf_op jit(solution)/shard_map/reduce_scatter | solution.py:286
  658.9 133.7 %reduce-scatter.15.cloned.1.call-start = ((), (), s32[]{:S(2)}) async-start(), calls=%async_computation.13 | async-start | bytes 5898240 | tf_op jit(solution)/shard_map/reduce_scatter | solution.py:298
  667.1 185.5 %reduce-scatter.17.cloned.1.call-start = ((), (), s32[]{:S(2)}) async-start(), calls=%async_computation.14 | async-start | bytes 5898240 | tf_op jit(solution)/shard_map/reduce_scatter | solution.py:304
  674.6 273.0 %all-reduce.23.cloned.1.call-start = ((), (), s32[]{:S(2)}) async-start(), calls=%async_computation.18 | async-start | bytes 7667712 | tf_op jit(solution)/shard_map/psum | solution.py:318
  703.4 150.6 %copy-start.17 = (bf16[192]{0:T(256)(128)(2,1)S(1)}, bf16[192]{0:T(256)(128)(2,1)}, u32[]{:S(2)}) copy-start(bf16[192]{0:T(256)(128)(2,1)} %param.35) | copy-start | bytes 1156
  856.1 37.7 %copy-start.2 = (f32[512,768]{1,0:T(8,128)S(1)}, f32[512,768]{1,0:T(8,128)}, u32[]{:S(2)}) copy-start(f32[512,768]{1,0:T(8,128)} %copy-done.1) | copy-start | bytes 4718596
  947.6 3.0 copy-start.9
  950.7 1.7 copy-start.10
  952.3 1.6 copy-start.11
Sparse Core Ops, SparseCore 0:
  9.9 50.0 all-gather.7
  67.7 65.1 all-gather.11
  135.0 63.2 all-gather.9
  200.1 25.9 all-gather.13
  227.7 57.1 all-gather.15
  286.6 57.0 all-gather.17
  496.1 69.7 reduce-scatter.18
  568.2 68.1 reduce-scatter.20
  655.5 45.5 reduce-scatter.22
  703.9 28.5 reduce-scatter.12
  735.5 57.0 reduce-scatter.14
  795.4 57.0 reduce-scatter.16
  855.8 91.8 all-reduce.22
where the time goes:
time: 970 us; the launch traced here: 961 us
  waiting for transfers between devices  527 us (54%)
  matrix products  222 us (23%)
  local copies, waits for them, and re-layouts  98.2 us (10%)
  blocking collectives  68.6 us (7%)
  other arithmetic  27.7 us (3%)
  between operations  16.5 us (2%)
    unnamed x16, waiting for transfers between devices  145 us
    unnamed x81, local copies, waits for them, and re-layouts  80.3 us
    reduce_scatter x1, waiting for transfers between devices, on_device(): lax.psum_scatter(grad_inner_weight.astype(jnp.bfloat16), 'seq', scatter_d...  60.1 us
    reduce_scatter x1, waiting for transfers between devices, on_device(): lax.psum_scatter(grad_outer_weight.astype(jnp.bfloat16), 'seq', scatter_d...  60 us
    all_gather x1, waiting for transfers between devices, on_device(): key_part = lax.all_gather(keys_low, 'ctx', axis=1, tiled=True)  58.8 us
    psum x1, waiting for transfers between devices, on_device(): lax.psum(owned[0].astype(jnp.bfloat16), 'ctx').astype(jnp.float32)  47.9 us
    all_gather x1, waiting for transfers between devices, on_device(): lax.all_gather(outer_weight, 'seq', axis=0, tiled=True)  39 us
    all_gather x1, waiting for transfers between devices, on_device(): value_part = lax.all_gather(values_low, 'ctx', axis=1, tiled=True)  36.3 us
  transfers between devices with their start and end apart: 13, of which 12 were waited for; matrix products, arithmetic and copies ran while one was open for 17% of the time, Pallas kernels for 0%

commit v1 on v0

--- a/solution.py
+++ b/solution.py
@@ -315,7 +315,7 @@
         ).astype(jnp.float32),
     )
     summed = (
-        lax.psum(owned[0].astype(jnp.bfloat16), "ctx").astype(jnp.float32),
+        jnp.sum(lax.all_gather(owned[0].astype(jnp.bfloat16), "ctx"), axis=0).astype(jnp.float32),
         lax.psum(owned[1].astype(jnp.bfloat16), "ctx").astype(jnp.float32),
         lax.psum(owned[2].astype(jnp.bfloat16), "ctx").astype(jnp.float32),
         lax.psum(owned[3].astype(jnp.bfloat16), "ctx").astype(jnp.float32),

time: 970 us -> 1000 us (1.031)
  waiting for transfers between devices: 527 us -> 558 us
    reduce_scatter x0 -> x1, waiting for transfers between devices: none -> 50.1 us  [on_device(): lax.psum_scatter(grad_qkv_weight.astype(jnp.bfloat16), 'seq', scatter_dim...]
    unnamed x16, waiting for transfers between devices: 145 us -> 99.4 us
    all_gather x0 -> x1, waiting for transfers between devices: none -> 23.4 us  [on_device(): lax.all_gather(owned[0].astype(jnp.bfloat16), 'ctx')]
    psum x1, waiting for transfers between devices: 47.9 us -> 69.6 us  [on_device(): lax.psum(owned[3].astype(jnp.bfloat16), 'ctx').astype(jnp.float32)]
    reduce_scatter x1, waiting for transfers between devices: 29 us -> 11.2 us  [on_device(): lax.psum_scatter(grad_out_weight.astype(jnp.bfloat16), 'seq', scatter_dim...]
    unnamed x81 -> x79, local copies, waits for them, and re-layouts: 80.3 us -> 77.6 us
  transfers between devices with their start and end apart: 13 -> 14, of which waited for: 12 -> 13; matrix products, arithmetic and copies ran while one was open for 17% -> 18% of each run, Pallas kernels for 0% -> 0%
where the time goes in v1:
time: 1000 us; the launch traced here: 995 us
  waiting for transfers between devices  558 us (56%)
  matrix products  221 us (22%)
  local copies, waits for them, and re-layouts  95.6 us (10%)
  blocking collectives  68.7 us (7%)
  other arithmetic  33.4 us (3%)
  between operations  16.5 us (2%)
    unnamed x16, waiting for transfers between devices  99.4 us
    unnamed x79, local copies, waits for them, and re-layouts  77.6 us
    psum x1, waiting for transfers between devices, on_device(): lax.psum(owned[3].astype(jnp.bfloat16), 'ctx').astype(jnp.float32)  69.6 us
    reduce_scatter x1, waiting for transfers between devices, on_device(): lax.psum_scatter(grad_outer_weight.astype(jnp.bfloat16), 'seq', scatter_d...  60.1 us
    reduce_scatter x1, waiting for transfers between devices, on_device(): lax.psum_scatter(grad_inner_weight.astype(jnp.bfloat16), 'seq', scatter_d...  59.9 us
    all_gather x1, waiting for transfers between devices, on_device(): key_part = lax.all_gather(keys_low, 'ctx', axis=1, tiled=True)  58.8 us
    reduce_scatter x1, waiting for transfers between devices, on_device(): lax.psum_scatter(grad_qkv_weight.astype(jnp.bfloat16), 'seq', scatter_dim...  50.1 us
    all_gather x1, waiting for transfers between devices, on_device(): lax.all_gather(outer_weight, 'seq', axis=0, tiled=True)  39 us
  transfers between devices with their start and end apart: 14, of which 13 were waited for; matrix products, arithmetic and copies ran while one was open for 18% of the time, Pallas kernels for 0%

profile of v1, /device:TPU:0, one launch (start us, length us, event | category | flops | bytes accessed | tf_op | source)
XLA Modules:
  0.0 995.4 jit_solution(7667257408375620933)
XLA Ops:
  15.8 17.8 %all-reduce.20 = (bf16[768]{0:T(1024)(128)(2,1)S(1)}, bf16[768]{0:T(1024)(128)(2,1)S(1)}, bf16[768]{0:T(1024)(128)(2,1)S(1)}, bf16[768]{0:T(1024)(128)(2,1)S(1)}...) all-reduce(bf16[768]{0:T(1024)(128)(2,1)S(1)} %dynamic-update-slice, ...), channel_id=1, replica_groups=mesh['seq'=4,'ctx'=8] {'seq'}, use_global_device_ids=true, to_apply=%add.2 | all-reduce | flops 5376 | bytes 21504
  33.7 26.3 %all-gather.10.cloned.1.call-done = bf16[768,2304]{1,0:T(8,128)(2,1)} async-done(((bf16[192,2304]{1,0:T(8,128)(2,1)}), bf16[768,2304]{1,0:T(8,128)(2,1)}) %all-gather.10.cloned.1.call-update) | async-done | bytes 3538960 | tf_op jit(solution)/shard_map/all_gather | solution.py:88
  60.0 4.3 fusion.86
  72.2 11.9 %all_gather.66 = bf16[4,1024]{1,0:T(4,128)(2,1)S(1)} all-gather(bf16[4,128]{1,0:T(4,128)(2,1)S(1)} %convert_element_type.238), channel_id=1, replica_groups=mesh['seq'=4,'ctx'=8] {'ctx'}, dimensions={1}, use_global_device_ids=true | all-gather | bytes 9216 | tf_op jit(solution)/shard_map/all_gather | solution.py:143
  84.1 8.2 all-gather.1
  96.5 36.3 %all-gather.14.cloned.1.call-done = bf16[4,1024,768]{1,2,0:T(8,128)(2,1)} async-done(((bf16[4,128,768]{1,2,0:T(8,128)(2,1)}), bf16[4,1024,768]{1,2,0:T(8,128)(2,1)}) %all-gather.14.cloned.1.call-update) | async-done | bytes 6291472 | tf_op jit(solution)/shard_map/all_gather | solution.py:142
  132.9 6.7 copy.56
  139.6 58.8 %all-gather.12.cloned.1.call-done = bf16[4,1024,768]{1,2,0:T(8,128)(2,1)} async-done(((bf16[4,128,768]{1,2,0:T(8,128)(2,1)}), bf16[4,1024,768]{1,2,0:T(8,128)(2,1)}) %all-gather.12.cloned.1.call-update) | async-done | bytes 6291472 | tf_op jit(solution)/shard_map/all_gather | solution.py:141
  198.4 6.7 copy.55
  205.1 51.8 %while.30 = (s32[]{:T(128)}, f32[12,4,128]{2,1,0:T(4,128)S(1)}, f32[12,4,128]{2,1,0:T(4,128)S(1)}, f32[12,4,128,64]{2,1,3,0:T(4,128)S(1)}, bf16[12,4,128,64]{2,3...) while((s32[]{:T(128)}, f32[12,4,128]{2,1,0:T(4,128)S(1)}, ...), condition=%wide.region_3.4_spmd.clone, body=%wide.region_0.3_spmd.clone.sunk | while | flops 142641664 | bytes 7852653 | solution.py:165
  258.0 2.6 fusion.83
  261.0 23.9 %all-gather.18.cloned.1.call-done = bf16[768,3072]{1,0:T(8,128)(2,1)} async-done(((bf16[192,3072]{1,0:T(8,128)(2,1)}), bf16[768,3072]{1,0:T(8,128)(2,1)}) %all-gather.18.cloned.1.call-update) | async-done | bytes 4718608 | tf_op jit(solution)/shard_map/all_gather | solution.py:95
  284.9 19.8 %multiply_convert_fusion.1 = (bf16[512,3072]{1,0:T(8,128)(2,1)}, f32[512,3072]{1,0:T(8,128)}, f32[512,3072]{1,0:T(8,128)}) fusion(f32[3072]{0:T(1024)S(1)} %bitcast.239, bf16[768,3072]{1,0:T(8,128)(2,1)} %all-gather.18.cloned.1.call-done, f32[512,768]{1,0:T(8,128)S(1)} %get-tuple-element.312, f32[768]{0:T(1024)S(1)} %convert_element_type.246, ...), kind=kOutput, calls=%fused_computation.66 | convolution fusion | flops 2521694208 | bytes 22042624 | tf_op jit(solution)/shard_map/dot_general | solution.py:183
  304.7 39.0 %all-gather.20.cloned.1.call-done = bf16[3072,768]{1,0:T(8,128)(2,1)} async-done(((bf16[768,768]{1,0:T(8,128)(2,1)}), bf16[3072,768]{1,0:T(8,128)(2,1)}) %all-gather.20.cloned.1.call-update) | async-done | bytes 4718608 | tf_op jit(solution)/shard_map/all_gather | solution.py:97
  343.7 6.5 fusion.84
  353.2 9.2 fusion.85
  362.4 5.1 multiply_reduce_fusion
  375.0 103.5 %while.31 = (s32[]{:T(128)}, bf16[12,4,128,64]{2,3,1,0:T(8,128)(2,1)}, bf16[12,4,1024,64]{2,3,0,1:T(8,128)(2,1)}, bf16[12,4,1024,64]{2,3,0,1:T(8,128)(2,1)}, bf1...) while((s32[]{:T(128)}, ...), condition=%wide.region_14.15_spmd.clone, body=%wide.region_13.14_spmd.clone.sunk | while | flops 340033536 | bytes 13657221 | solution.py:244
  399.0 2.2 fusion.138
  416.2 2.2 fusion.138
  433.4 2.2 fusion.138
  442.0 2.2 fusion.138
  459.1 2.2 fusion.138
  467.7 2.2 fusion.138
  476.3 2.2 fusion.138
  478.5 10.8 %copy.69 = bf16[4,1024,768]{2,0,1:T(4,128)(2,1)} copy(bf16[4,1024,768]{1,2,0:T(8,128)(2,1)} %bitcast.221) | data formatting | bytes 12582912
  489.3 6.9 copy.99
  496.3 11.0 %copy.71 = bf16[4,1024,768]{2,0,1:T(4,128)(2,1)} copy(bf16[4,1024,768]{1,2,0:T(8,128)(2,1)} %bitcast.222) | data formatting | bytes 12582912
  507.2 7.0 copy.101
  515.3 3.2 convolution_convert_fusion.3
  518.6 7.4 convolution_convert_fusion.1
  526.1 7.2 convolution_convert_fusion
  536.3 29.8 %reduce-scatter.19.cloned.1.call-done = bf16[128,3072]{1,0:T(8,128)(2,1)} async-done(((bf16[1024,3072]{1,0:T(8,128)(2,1)}), bf16[128,3072]{1,0:T(8,128)(2,1)}) %reduce-scatter.19.cloned.1.call-update) | async-done | bytes 786448
  569.5 67.2 %reduce-scatter.21.cloned.1.call-done = bf16[128,3072]{1,0:T(8,128)(2,1)} async-done(((bf16[1024,3072]{1,0:T(8,128)(2,1)}), bf16[128,3072]{1,0:T(8,128)(2,1)}) %reduce-scatter.21.cloned.1.call-update) | async-done | bytes 786448
  640.0 2.2 bitcast_dynamic-update-slice_fusion.2
  644.4 5.6 fusion.54
  650.0 5.8 copy.73
  655.9 11.2 %reduce-scatter.13.cloned.1.call-done = bf16[192,768]{1,0:T(8,128)(2,1)} async-done(((bf16[768,768]{1,0:T(8,128)(2,1)}), bf16[192,768]{1,0:T(8,128)(2,1)}) %reduce-scatter.13.cloned.1.call-update) | async-done | bytes 294928 | tf_op jit(solution)/shard_map/reduce_scatter | solution.py:286
  667.1 59.9 %reduce-scatter.15.cloned.1.call-done = bf16[192,3072]{1,0:T(8,128)(2,1)} async-done(((bf16[768,3072]{1,0:T(8,128)(2,1)}), bf16[192,3072]{1,0:T(8,128)(2,1)}) %reduce-scatter.15.cloned.1.call-update) | async-done | bytes 1179664 | tf_op jit(solution)/shard_map/reduce_scatter | solution.py:298
  727.1 60.1 %reduce-scatter.17.cloned.1.call-done = bf16[768,768]{1,0:T(8,128)(2,1)} async-done(((bf16[3072,768]{1,0:T(8,128)(2,1)}), bf16[768,768]{1,0:T(8,128)(2,1)}) %reduce-scatter.17.cloned.1.call-update) | async-done | bytes 1179664 | tf_op jit(solution)/shard_map/reduce_scatter | solution.py:304
  787.3 50.1 %reduce-scatter.23.cloned.1.call-done = bf16[192,2304]{1,0:T(8,128)(2,1)} async-done(((bf16[768,2304]{1,0:T(8,128)(2,1)}), bf16[192,2304]{1,0:T(8,128)(2,1)}) %reduce-scatter.23.cloned.1.call-update) | async-done | bytes 884752 | tf_op jit(solution)/shard_map/reduce_scatter | solution.py:277
  840.6 69.6 %all-reduce.23.cloned.1.call-done = (bf16[192,768]{1,0:T(8,128)(2,1)}, bf16[192,3072]{1,0:T(8,128)(2,1)}, bf16[768,768]{1,0:T(8,128)(2,1)}) async-done(((bf16[192,768]{1,0:T(8,128)(2,1)}, bf16[192,3072]{1,0:T(8,128)(2,1)}, bf16[768,768]{1,0:T(8,128)(2,1)}), (bf16[192,768]{1,0:T(8,128)(2,1)}, bf16[192,3072]{1,0:T(8,128)(2,1)}, bf16[768,768]{1,0:T(8,128)(2,1)})) %all-reduce.23.cloned.1.call-update) | async-done | bytes 2654224 | tf_op jit(solution)/shard_map/psum | solution.py:321
  910.2 3.0 convert_element_type.286
  916.0 16.2 %all-reduce.19 = (bf16[768]{0:T(1024)(128)(2,1)S(1)}, bf16[768]{0:T(1024)(128)(2,1)S(1)}, bf16[768]{0:T(1024)(128)(2,1)S(1)}, bf16[768]{0:T(1024)(128)(2,1)S(1)}...) all-reduce(bf16[768]{0:T(1024)(128)(2,1)S(1)} %dynamic-update-slice, ...), channel_id=1, replica_groups=mesh['seq'=4,'ctx'=8] {'seq'}, use_global_device_ids=true, to_apply=%add.7 | all-reduce | flops 9984 | bytes 39936
  932.9 14.6 %all-reduce.17 = (bf16[192]{0:T(256)(128)(2,1)S(1)}, bf16[192]{0:T(256)(128)(2,1)S(1)}, bf16[192]{0:T(256)(128)(2,1)S(1)}, bf16[192]{0:T(256)(128)(2,1)S(1)}, bf...) all-reduce(bf16[192]{0:T(256)(128)(2,1)S(1)} %dynamic-slice.9, ...), channel_id=1, replica_groups=mesh['seq'=4,'ctx'=8] {'ctx'}, use_global_device_ids=true, to_apply=%region_21.22 | all-reduce | flops 2304 | bytes 9216 | tf_op jit(solution)/shard_map/psum | solution.py:319
  953.8 5.7 convolution_add_fusion.1
  959.5 23.4 %all-gather.22.cloned.1.call-done = bf16[1536,2304]{1,0:T(8,128)(2,1)} async-done(((bf16[192,2304]{1,0:T(8,128)(2,1)}), bf16[1536,2304]{1,0:T(8,128)(2,1)}) %all-gather.22.cloned.1.call-update) | async-done | bytes 7077904 | tf_op jit(solution)/shard_map/all_gather | solution.py:318
  982.9 4.4 reduce_sum.214
  (312 shorter events, 197.0 us)
Async XLA Ops:
  7.2 52.8 %all-gather.10.cloned.1.call-start = ((), (), s32[]{:S(2)}) async-start(), calls=%async_computation.6 | async-start | bytes 4423680 | tf_op jit(solution)/shard_map/all_gather | solution.py:88
  7.9 125.0 %all-gather.14.cloned.1.call-start = ((), (), s32[]{:S(2)}) async-start(), calls=%async_computation.8 | async-start | bytes 7077888 | tf_op jit(solution)/shard_map/all_gather | solution.py:142
  64.2 2.1 copy-start.5
  67.5 130.9 %all-gather.12.cloned.1.call-start = ((), (), s32[]{:S(2)}) async-start(), calls=%async_computation.7 | async-start | bytes 7077888 | tf_op jit(solution)/shard_map/all_gather | solution.py:141
  69.1 3.1 copy-start.12
  69.1 15.0 %copy-start.13 = (bf16[768]{0:T(1024)(128)(2,1)S(1)}, bf16[768]{0:T(1024)(128)(2,1)}, u32[]{:S(2)}) copy-start(bf16[768]{0:T(1024)(128)(2,1)} %param.31) | copy-start | bytes 4612
  69.1 23.2 %copy-start = (bf16[4,128,768]{2,1,0:T(8,128)(2,1)S(1)}, bf16[4,128,768]{2,1,0:T(8,128)(2,1)}, u32[]{:S(2)}) copy-start(bf16[4,128,768]{2,1,0:T(8,128)(2,1)} %param.21) | copy-start | bytes 2359300
  70.3 187.0 %all-gather.16.cloned.1.call-start = ((), (), s32[]{:S(2)}) async-start(), calls=%async_computation.9 | async-start | bytes 1474560 | tf_op jit(solution)/shard_map/all_gather | solution.py:91
  70.9 214.0 %all-gather.18.cloned.1.call-start = ((), (), s32[]{:S(2)}) async-start(), calls=%async_computation.10 | async-start | bytes 5898240 | tf_op jit(solution)/shard_map/all_gather | solution.py:95
  71.5 272.2 %all-gather.20.cloned.1.call-start = ((), (), s32[]{:S(2)}) async-start(), calls=%async_computation.11 | async-start | bytes 5898240 | tf_op jit(solution)/shard_map/all_gather | solution.py:97
  72.0 494.1 %reduce-scatter.19.cloned.1.call-start = ((), (), s32[]{:S(2)}) async-start(), calls=%async_computation.16 | async-start | bytes 7077888
  256.9 1.1 copy-start.4
  257.2 3.4 copy-start.6
  260.7 44.0 %copy-start.2 = (f32[512,768]{1,0:T(8,128)}, f32[512,768]{1,0:T(8,128)S(1)}, u32[]{:S(2)}) copy-start(f32[512,768]{1,0:T(8,128)S(1)} %get-tuple-element.312) | copy-start | bytes 4718596
  350.5 2.8 copy-start.14
  351.1 11.3 %slice-start = ((s8[4718592]{0:T(1024)(128)(4,1)}), s8[4194304]{0:T(1024)(128)(4,1)S(1)}, s32[]{:S(2)}) async-start(s8[4718592]{0:T(1024)(128)(4,1)} %bitcast.241), calls=%async_computation.20 | async-start | bytes 8388608
  351.7 10.7 %copy-start.8 = (f32[512,768]{1,0:T(8,128)}, f32[512,768]{1,0:T(8,128)S(1)}, u32[]{:S(2)}) copy-start(f32[512,768]{1,0:T(8,128)S(1)} %get-tuple-element.294) | copy-start | bytes 4718596
  353.2 9.2 copy-start.3
  353.2 9.2 slice-start.1
  367.6 1.7 copy-start.15
  368.1 1.2 copy-start.1
  496.2 140.5 %reduce-scatter.21.cloned.1.call-start = ((), (), s32[]{:S(2)}) async-start(), calls=%async_computation.17 | async-start | bytes 7077888
  514.2 1.1 copy-start.7
  514.2 152.9 %reduce-scatter.13.cloned.1.call-start = ((), (), s32[]{:S(2)}) async-start(), calls=%async_computation.12 | async-start | bytes 1474560 | tf_op jit(solution)/shard_map/reduce_scatter | solution.py:286
  518.6 208.5 %reduce-scatter.15.cloned.1.call-start = ((), (), s32[]{:S(2)}) async-start(), calls=%async_computation.13 | async-start | bytes 5898240 | tf_op jit(solution)/shard_map/reduce_scatter | solution.py:298
  526.1 261.1 %reduce-scatter.17.cloned.1.call-start = ((), (), s32[]{:S(2)}) async-start(), calls=%async_computation.14 | async-start | bytes 5898240 | tf_op jit(solution)/shard_map/reduce_scatter | solution.py:304
  533.3 304.1 %reduce-scatter.23.cloned.1.call-start = ((), (), s32[]{:S(2)}) async-start(), calls=%async_computation.18 | async-start | bytes 4423680 | tf_op jit(solution)/shard_map/reduce_scatter | solution.py:277
  640.0 4.4 copy-start.16
  655.9 183.1 %copy-start.17 = (bf16[192]{0:T(256)(128)(2,1)S(1)}, bf16[192]{0:T(256)(128)(2,1)}, u32[]{:S(2)}) copy-start(bf16[192]{0:T(256)(128)(2,1)} %param.35) | copy-start | bytes 1156
  655.9 254.3 %all-reduce.23.cloned.1.call-start = ((), (), s32[]{:S(2)}) async-start(), calls=%async_computation.19 | async-start | bytes 5308416 | tf_op jit(solution)/shard_map/psum | solution.py:321
  787.2 195.7 %all-gather.22.cloned.1.call-start = ((), (), s32[]{:S(2)}) async-start(), calls=%async_computation.15 | async-start | bytes 7962624 | tf_op jit(solution)/shard_map/all_gather | solution.py:318
  910.2 3.0 copy-start.9
  913.2 1.6 copy-start.10
  947.5 6.3 copy-start.11
Sparse Core Ops, SparseCore 0:
  9.9 50.0 all-gather.9
  67.7 65.1 all-gather.13
  135.0 63.2 all-gather.11
  200.1 25.9 all-gather.15
  227.7 57.1 all-gather.17
  286.6 57.0 all-gather.19
  496.3 69.7 reduce-scatter.18
  568.5 68.1 reduce-scatter.20
  640.2 26.9 reduce-scatter.12
  670.0 57.0 reduce-scatter.14
  730.1 57.0 reduce-scatter.16
  790.1 47.2 reduce-scatter.22
  840.0 70.1 all-reduce.22
  911.7 71.1 all-gather.21
